TPU v7x, 32 devices: a whole 2x2x4 slice. The times are simulated.
32 devices in a mesh: groups: 1, kcol: 16 (over z, y, x), qrow: 2 (over core).
Axes of the slice: x: 2, y: 2, z: 4, core: 2. Of those that a mesh axis runs over, the one named last changes fastest.
Arguments:
- queries: bfloat16 [128, 1024], P(('groups', 'kcol', 'qrow')), may hold values from -120 to 120
- key_value: bfloat16 [24576, 256], P(('groups', 'kcol')), may hold values from -6 to 6
- block_lists: int32 [1, 64], P('groups'), may hold values from 0 to 191, as said below
Outputs:
- attended: bfloat16 [128, 1024], P(('groups', 'kcol', 'qrow'))
Inputs may be any that keep to these rules, and one draw needn't show every extreme that they name: `block_lists`: row i names 64 distinct key blocks, none after block 191 + i (the block that holds query block i); it always names that block, the 11 blocks just before it, and block 0.
All inputs are finite; a program needn't handle non-finite values.
Results may differ from a plain program's by a relative error of at most 0.0065.
Values may be sent and summed in bfloat16 or wider, within the bound.
No kernel may reach another device: no remote copies, remote signals or barrier semaphores. Data moves between devices by JAX's collectives and lax.ppermute only.
A program may use at most 128 MiB of HBM per device.

v0:
```python
import math
import jax
import jax.numpy as jnp
from jax import lax
from jax.sharding import PartitionSpec as P

BLK = 128
masked_score = -1e30


def combined_all(part, axis, combine):
    gathered = jax.tree.map(lambda a: lax.all_gather(a, axis), part)

    def take(source):
        return jax.tree.map(lambda a: lax.dynamic_index_in_dim(a, source, 0, False), gathered)

    return lax.fori_loop(
        1, lax.axis_size(axis), lambda source, state: combine(state, take(source)), take(0)
    )


def partial_softmax(query_tile, key_rows, value_rows, visible):
    score_scale = 1.0 / math.sqrt(key_rows.shape[1])
    scores = (
        jnp.einsum("thd,kd->htk", query_tile, key_rows, preferred_element_type=jnp.float32)
        * score_scale
    )
    scores = jnp.where(visible[None], scores, masked_score)
    row_max = jnp.max(scores, axis=-1)
    weights = jnp.where(visible[None], jnp.exp(scores - row_max[..., None]), 0.0)
    row_total = jnp.sum(weights, axis=-1)
    numerator = jnp.einsum(
        "htk,kd->thd", weights.astype(jnp.bfloat16), value_rows, preferred_element_type=jnp.float32
    )
    return (jnp.transpose(row_max), jnp.transpose(row_total), numerator)


def combine_partials(left_part, right_part):
    max_left, total_left, numer_left = left_part
    max_right, total_right, numer_right = right_part
    row_max = jnp.maximum(max_left, max_right)
    scale_left = jnp.exp(max_left - row_max)
    scale_right = jnp.exp(max_right - row_max)
    return (
        row_max,
        total_left * scale_left + total_right * scale_right,
        numer_left * scale_left[..., None] + numer_right * scale_right[..., None],
    )


def per_device(queries, key_value, block_lists):
    column_count = lax.axis_size("kcol")
    column = lax.axis_index("kcol")
    row_count = lax.axis_size("qrow")
    row_index = lax.axis_index("qrow")
    tok_dev = queries.shape[0]
    feature_count = queries.shape[1]
    head_dim = key_value.shape[1] // 2
    head_count = feature_count // head_dim
    stored = key_value.shape[0] // BLK
    all_blocks = stored * column_count
    gathered = lax.all_gather(queries, "kcol", axis=0, tiled=True)
    gathered_rows = gathered.shape[0]
    tile_rows = BLK // row_count
    query_blocks = gathered_rows // tile_rows
    offset = (all_blocks - query_blocks) * BLK
    gather_pos = jnp.arange(gathered_rows, dtype=jnp.int32)
    token_index = (gather_pos // tok_dev * row_count + row_index) * tok_dev + gather_pos % tok_dev
    query_pos = (offset + token_index).reshape(query_blocks, tile_rows)
    query_tiles = gathered.reshape(query_blocks, tile_rows, head_count, head_dim)
    block_ids = column * stored + jnp.arange(stored, dtype=jnp.int32)
    key_pos = column * stored * BLK + jnp.arange(stored * BLK, dtype=jnp.int32)
    key_rows = key_value[:, :head_dim]
    value_rows = key_value[:, head_dim:]

    def one_block(inputs):
        query_tile, positions, listed = inputs
        listed_here = jnp.any(listed[:, None] == block_ids[None, :], axis=0)
        usable = jnp.repeat(listed_here, BLK, total_repeat_length=stored * BLK)
        visible = usable[None, :] & (key_pos[None, :] <= positions[:, None])
        return partial_softmax(query_tile, key_rows, value_rows, visible)

    row_max, row_total, numerator = lax.map(one_block, (query_tiles, query_pos, block_lists))
    row_max = row_max.reshape(gathered_rows, head_count)
    row_total = row_total.reshape(gathered_rows, head_count)
    numerator = numerator.reshape(gathered_rows, head_count, head_dim)
    merged = combined_all((row_max, row_total, numerator), "kcol", combine_partials)
    first_row = column * tok_dev
    summed_total = lax.dynamic_slice_in_dim(merged[1], first_row, tok_dev, 0)
    summed_numer = lax.dynamic_slice_in_dim(merged[2], first_row, tok_dev, 0)
    attended = summed_numer / summed_total[..., None]
    return attended.reshape(tok_dev, feature_count).astype(jnp.bfloat16)


def solution(mesh):
    placed = (P(("groups", "kcol", "qrow"), None), P(("groups", "kcol"), None), P("groups", None))
    return jax.shard_map(
        per_device,
        mesh=mesh,
        in_specs=placed,
        out_specs=P(("groups", "kcol", "qrow"), None),
        check_vma=False,
    )
```

profile of v0, /device:TPU:0, one launch (start us, length us, event | category | flops | bytes accessed | tf_op | source)
XLA Modules:
  0.0 169.5 jit_solution(10916630586948243898)
XLA Ops:
  6.6 0.8 compare_reduce_fusion.5
  7.4 0.7 fusion.37
  8.1 43.3 %all-gather.3 = bf16[16,4,1024]{2,1,0:T(4,128)(2,1)S(1)} all-gather(bf16[1,4,1024]{2,1,0:T(4,128)(2,1)} %bitcast.104), channel_id=1, replica_groups=mesh['groups'=1,'kcol'=16,'qrow'=2] {'kcol'}, dimensions={0}, use_global_device_ids=true | all-gather | bytes 139264 | tf_op jit(solution)/shard_map/all_gather | solution.py:62
  51.5 4.5 %select_reduce_fusion = (pred[1536]{0:T(1024)(128)(4,1)S(1)}, pred[1536]{0:T(1024)(128)(4,1)S(1)}, pred[1536]{0:T(1024)(128)(4,1)S(1)}, pred[1536]{0:T(1024)(128...) fusion(pred[]{:T(512)} %bitcast.11, pred[]{:T(512)} %bitcast.12, pred[]{:T(512)} %bitcast.13, ...), kind=kLoop, calls=%fused_computation.28 | loop fusion | flops 29184 | bytes 21511 | tf_op jit(solution)/shard_map/while/body/eval_jaxpr/jit(_take)/gather | solution.py:79
  56.0 3.2 %fusion.29 = pred[1536]{0:T(1024)(128)(4,1)S(1)} fusion(pred[1536]{0:T(1024)(128)(4,1)S(1)} %get-tuple-element.267, pred[1536]{0:T(1024)(128)(4,1)S(1)} %get-tuple-element.266, pred[1536]{0:T(1024)(128)(4,1)S(1)} %get-tuple-element.265, pred[1536]{0:T(1024)(128)(4,1)S(1)} %get-tuple-element.263, pred[1536]{0:T(1024)(128)(4,1)S(1)} %get-tuple-element.264, ...), kind=kLoop, calls=%fused_computation.47 | loop fusion | flops 21504 | bytes 10757 | tf_op jit(solution)/shard_map/while/body/eval_jaxpr/jit(_take)/select_n | solution.py:79
  59.2 0.1 compare_and_fusion
  59.4 1.7 %fusion.38 = (f32[8,64]{1,0:T(8,128)S(1)}, f32[8,64,1536]{2,1,0:T(8,128)S(1)}) fusion(bf16[64,8,128]{2,1,0:T(8,128)(2,1)S(1)} %squeeze.51, bf16[1536,256]{1,0:T(8,128)(2,1)} %param.8, pred[64,1536]{1,0:T(8,128)(4,1)S(1)} %compare_and_fusion), kind=kOutput, calls=%fused_computation.65 | convolution fusion | flops 203685376 | bytes 3770368 | tf_op jit(solution)/shard_map/while/body/eval_jaxpr/thd,kd->htk/dot_general | solution.py:25
  61.1 1.3 fusion.13
  62.5 0.7 fusion.7
  63.2 36.2 %all-gather.5 = f32[16,64,8]{1,2,0:T(8,128)S(1)} all-gather(f32[1,64,8]{1,2,0:T(8,128)S(1)} %bitcast.103), channel_id=3, replica_groups=mesh['groups'=1,'kcol'=16,'qrow'=2] {'kcol'}, dimensions={0}, use_global_device_ids=true | all-gather | bytes 34816 | tf_op jit(solution)/shard_map/all_gather | solution.py:12
  99.4 39.0 %all-gather.4 = f32[16,64,8]{1,2,0:T(8,128)S(1)} all-gather(f32[1,64,8]{1,2,0:T(8,128)S(1)} %bitcast.102), channel_id=2, replica_groups=mesh['groups'=1,'kcol'=16,'qrow'=2] {'kcol'}, dimensions={0}, use_global_device_ids=true | all-gather | bytes 34816 | tf_op jit(solution)/shard_map/all_gather | solution.py:12
  138.4 1.0 slice.53
  139.4 0.2 copy.24
  139.6 22.3 %while.26 = (s32[]{:T(128)}, f32[64,8]{0,1:T(8,128)S(1)}, f32[64,8]{0,1:T(8,128)S(1)}, f32[64,8,128]{2,1,0:T(8,128)S(1)}, f32[16,64,8]{1,2,0:T(8,128)S(1)}, /*in...) while((s32[]{:T(128)}, f32[64,8]{0,1:T(8,128)S(1)}, ...), condition=%wide.region_4.5_spmd, body=%wide.region_3.4_spmd.sunk | while | flops 199685 | bytes 1339535 | solution.py:17
  139.6 0.1 copy.48
  139.8 1.0 constant_dynamic-slice_fusion.3
  140.7 0.3 fusion.42
  141.1 0.1 copy.48
  141.3 1.0 constant_dynamic-slice_fusion.3
  142.2 0.3 fusion.42
  142.6 0.1 copy.48
  142.7 1.0 constant_dynamic-slice_fusion.3
  143.7 0.3 fusion.42
  144.2 1.0 constant_dynamic-slice_fusion.3
  145.2 0.3 fusion.42
  145.7 1.0 constant_dynamic-slice_fusion.3
  146.7 0.3 fusion.42
  147.2 1.0 constant_dynamic-slice_fusion.3
  148.2 0.3 fusion.42
  148.7 1.0 constant_dynamic-slice_fusion.3
  149.7 0.3 fusion.42
  150.2 1.0 constant_dynamic-slice_fusion.3
  151.1 0.3 fusion.42
  151.7 1.0 constant_dynamic-slice_fusion.3
  152.6 0.3 fusion.42
  153.1 1.0 constant_dynamic-slice_fusion.3
  154.1 0.3 fusion.42
  154.6 1.0 constant_dynamic-slice_fusion.3
  155.6 0.3 fusion.42
  156.1 1.0 constant_dynamic-slice_fusion.3
  157.1 0.3 fusion.42
  157.6 1.0 constant_dynamic-slice_fusion.3
  158.6 0.3 fusion.42
  159.1 1.0 constant_dynamic-slice_fusion.3
  160.1 0.3 fusion.42
  160.6 1.0 constant_dynamic-slice_fusion.3
  161.5 0.3 fusion.42
  162.1 0.6 copy.43
  (57 shorter events, 2.9 us)
Async XLA Ops:
  6.5 131.9 %all-gather.8.cloned.1.call-start = ((), (), s32[]{:S(2)}) async-start(), calls=%async_computation | async-start | bytes 4456448 | tf_op jit(solution)/shard_map/all_gather | solution.py:12
  51.5 9.6 %copy-start = (bf16[1536,256]{1,0:T(8,128)(2,1)S(1)}, bf16[1536,256]{1,0:T(8,128)(2,1)}, u32[]{:S(2)}) copy-start(bf16[1536,256]{1,0:T(8,128)(2,1)} %param.8) | copy-start | bytes 2359300
Sparse Core Ops, SparseCore 0:
  62.6 72.8 all-gather.7
where the time goes:
time: 170 us
  blocking collectives  119 us (70%)
  local copies, waits for them, and re-layouts  19.7 us (12%)
  other arithmetic  14.2 us (8%)
  between operations  13.5 us (8%)
  matrix products  3.06 us (2%)
    all_gather x2, blocking collectives, combined_all(): gathered = jax.tree.map(lambda a: lax.all_gather(a, axis), part)  75.2 us
    all_gather x1, blocking collectives, per_device(): gathered = lax.all_gather(queries, 'kcol', axis=0, tiled=True)  43.3 us
    dynamic_slice x18, local copies, waits for them, and re-layouts, take(): lax.dynamic_index_in_dim(a, source, 0, False)  15.5 us
    gather x1, other arithmetic, one_block(): usable = jnp.repeat(listed_here, BLK, total_repeat_length=stored * BLK)  4.49 us
    add x15, other arithmetic, combine_partials(): numer_left * scale_left[..., None] + numer_right * scale_right[..., None]  4.46 us
  transfers between devices with their start and end apart: 1, of which 0 were waited for; matrix products, arithmetic and copies ran while one was open for 0% of the time, Pallas kernels for 0%

commit v1 on v0

--- a/solution.py
+++ b/solution.py
@@ -59,7 +59,15 @@
     head_count = feature_count // head_dim
     stored = key_value.shape[0] // BLK
     all_blocks = stored * column_count
-    gathered = lax.all_gather(queries, "kcol", axis=0, tiled=True)
+    chips = lax.axis_size("kcol")
+    current_arr = sorted(((jj, (jj + 1) % chips) for jj in range(chips)))
+    t1 = queries
+    buffer = [t1]
+    for h in range(1, chips):
+        t1 = lax.ppermute(t1, "kcol", current_arr)
+        buffer.insert(0, t1)
+    v_next = jnp.concatenate(buffer, 0)
+    gathered = jnp.roll(v_next, (lax.axis_index("kcol") + 1) * queries.shape[0], 0)
     gathered_rows = gathered.shape[0]
     tile_rows = BLK // row_count
     query_blocks = gathered_rows // tile_rows

time: 170 us -> 230 us (1.35)
  waiting for transfers between devices: 0.02 us -> 97.9 us
  blocking collectives: 119 us -> 75.4 us
  other arithmetic: 14.2 us -> 28 us
  local copies, waits for them, and re-layouts: 19.7 us -> 7.07 us
  starting transfers between devices: 0.01 us -> 3.01 us
    ppermute x0 -> x15, waiting for transfers between devices: none -> 97.9 us  [per_device(): t1 = lax.ppermute(t1, 'kcol', current_arr)]
    all_gather x1 -> x0, blocking collectives: 43.3 us -> none  [per_device(): gathered = lax.all_gather(queries, 'kcol', axis=0, tiled=True)]
    dynamic_slice x18 -> x3, local copies, waits for them, and re-layouts: 15.5 us -> 0.97 us  [take(): lax.dynamic_index_in_dim(a, source, 0, False)]
    add x15, other arithmetic: 4.46 us -> 18.1 us  [combine_partials(): numer_left * scale_left[..., None] + numer_right * scale_right[..., None]]
    ppermute x0 -> x15, starting transfers between devices: none -> 3 us  [per_device(): t1 = lax.ppermute(t1, 'kcol', current_arr)]
  transfers between devices with their start and end apart: 1 -> 16, of which waited for: 0 -> 15; matrix products, arithmetic and copies ran while one was open for 0% -> 5% of each run, Pallas kernels for 0% -> 0%
where the time goes in v1:
time: 230 us; the launch traced here: 229 us
  waiting for transfers between devices  97.9 us (43%)
  blocking collectives  75.4 us (33%)
  other arithmetic  28 us (12%)
  between operations  13.5 us (6%)
  local copies, waits for them, and re-layouts  7.07 us (3%)
  matrix products  3.45 us (2%)
  starting transfers between devices  3.01 us (1%)
    ppermute x15, waiting for transfers between devices, per_device(): t1 = lax.ppermute(t1, 'kcol', current_arr)  97.9 us
    all_gather x2, blocking collectives, combined_all(): gathered = jax.tree.map(lambda a: lax.all_gather(a, axis), part)  75.4 us
    add x15, other arithmetic, combine_partials(): numer_left * scale_left[..., None] + numer_right * scale_right[..., None]  18.1 us
  transfers between devices with their start and end apart: 16, of which 15 were waited for; matrix products, arithmetic and copies ran while one was open for 5% of the time, Pallas kernels for 0%

profile of v1, /device:TPU:0, one launch (start us, length us, event | category | flops | bytes accessed | tf_op | source)
XLA Modules:
  0.0 228.7 jit_solution(2490018167699995257)
XLA Ops:
  6.5 3.0 %collective-permute-start = (bf16[4,1024]{1,0:T(4,128)(2,1)}, bf16[4,1024]{1,0:T(4,128)(2,1)S(1)}, u32[]{:S(2)}, u32[]{:S(2)}) collective-permute-start(bf16[4,1024]{1,0:T(4,128)(2,1)} %param.7), channel_id=1, source_target_pairs={{0,2},{2,4},{4,6},{6,8},{8,10},{10,12},{12,14},{14,16},{16,18},{18... | collective-permute-start | bytes 24584 | tf_op jit(solution)/shard_map/ppermute | solution.py:67
  9.5 5.8 %collective-permute-done = bf16[4,1024]{1,0:T(4,128)(2,1)S(1)} collective-permute-done((bf16[4,1024]{1,0:T(4,128)(2,1)}, bf16[4,1024]{1,0:T(4,128)(2,1)S(1)}, u32[]{:S(2)}, u32[]{:S(2)}) %collective-permute-start) | collective-permute-done | bytes 8224 | tf_op jit(solution)/shard_map/ppermute | solution.py:67
  15.3 7.2 %collective-permute-done.1 = bf16[4,1024]{1,0:T(4,128)(2,1)S(1)} collective-permute-done((bf16[4,1024]{1,0:T(4,128)(2,1)S(1)}, bf16[4,1024]{1,0:T(4,128)(2,1)S(1)}, u32[]{:S(2)}, u32[]{:S(2)}) %collective-permute-start.1) | collective-permute-done | bytes 8224 | tf_op jit(solution)/shard_map/ppermute | solution.py:67
  22.6 7.2 %collective-permute-done.2 = bf16[4,1024]{1,0:T(4,128)(2,1)S(1)} collective-permute-done((bf16[4,1024]{1,0:T(4,128)(2,1)S(1)}, bf16[4,1024]{1,0:T(4,128)(2,1)S(1)}, u32[]{:S(2)}, u32[]{:S(2)}) %collective-permute-start.2) | collective-permute-done | bytes 8224 | tf_op jit(solution)/shard_map/ppermute | solution.py:67
  29.8 7.2 %collective-permute-done.3 = bf16[4,1024]{1,0:T(4,128)(2,1)S(1)} collective-permute-done((bf16[4,1024]{1,0:T(4,128)(2,1)S(1)}, bf16[4,1024]{1,0:T(4,128)(2,1)S(1)}, u32[]{:S(2)}, u32[]{:S(2)}) %collective-permute-start.3) | collective-permute-done | bytes 8224 | tf_op jit(solution)/shard_map/ppermute | solution.py:67
  37.1 7.2 %collective-permute-done.4 = bf16[4,1024]{1,0:T(4,128)(2,1)S(1)} collective-permute-done((bf16[4,1024]{1,0:T(4,128)(2,1)S(1)}, bf16[4,1024]{1,0:T(4,128)(2,1)S(1)}, u32[]{:S(2)}, u32[]{:S(2)}) %collective-permute-start.4) | collective-permute-done | bytes 8224 | tf_op jit(solution)/shard_map/ppermute | solution.py:67
  44.3 7.2 %collective-permute-done.5 = bf16[4,1024]{1,0:T(4,128)(2,1)S(1)} collective-permute-done((bf16[4,1024]{1,0:T(4,128)(2,1)S(1)}, bf16[4,1024]{1,0:T(4,128)(2,1)S(1)}, u32[]{:S(2)}, u32[]{:S(2)}) %collective-permute-start.5) | collective-permute-done | bytes 8224 | tf_op jit(solution)/shard_map/ppermute | solution.py:67
  51.6 7.2 %collective-permute-done.6 = bf16[4,1024]{1,0:T(4,128)(2,1)S(1)} collective-permute-done((bf16[4,1024]{1,0:T(4,128)(2,1)S(1)}, bf16[4,1024]{1,0:T(4,128)(2,1)S(1)}, u32[]{:S(2)}, u32[]{:S(2)}) %collective-permute-start.6) | collective-permute-done | bytes 8224 | tf_op jit(solution)/shard_map/ppermute | solution.py:67
  58.8 0.8 compare_reduce_fusion.5
  59.7 6.4 %collective-permute-done.7 = bf16[4,1024]{1,0:T(4,128)(2,1)S(1)} collective-permute-done((bf16[4,1024]{1,0:T(4,128)(2,1)S(1)}, bf16[4,1024]{1,0:T(4,128)(2,1)S(1)}, u32[]{:S(2)}, u32[]{:S(2)}) %collective-permute-start.7) | collective-permute-done | bytes 8224 | tf_op jit(solution)/shard_map/ppermute | solution.py:67
  66.1 0.7 fusion.35
  66.8 6.5 %collective-permute-done.8 = bf16[4,1024]{1,0:T(4,128)(2,1)S(1)} collective-permute-done((bf16[4,1024]{1,0:T(4,128)(2,1)S(1)}, bf16[4,1024]{1,0:T(4,128)(2,1)S(1)}, u32[]{:S(2)}, u32[]{:S(2)}) %collective-permute-start.8) | collective-permute-done | bytes 8224 | tf_op jit(solution)/shard_map/ppermute | solution.py:67
  73.3 7.2 %collective-permute-done.9 = bf16[4,1024]{1,0:T(4,128)(2,1)S(1)} collective-permute-done((bf16[4,1024]{1,0:T(4,128)(2,1)S(1)}, bf16[4,1024]{1,0:T(4,128)(2,1)S(1)}, u32[]{:S(2)}, u32[]{:S(2)}) %collective-permute-start.9) | collective-permute-done | bytes 8224 | tf_op jit(solution)/shard_map/ppermute | solution.py:67
  80.6 4.4 %select_reduce_fusion = (pred[1536]{0:T(1024)(128)(4,1)S(1)}, pred[1536]{0:T(1024)(128)(4,1)S(1)}, pred[1536]{0:T(1024)(128)(4,1)S(1)}, pred[1536]{0:T(1024)(128...) fusion(pred[]{:T(512)} %bitcast.11, pred[]{:T(512)} %bitcast.12, pred[]{:T(512)} %bitcast.13, ...), kind=kLoop, calls=%fused_computation.26 | loop fusion | flops 29184 | bytes 21511 | tf_op jit(solution)/shard_map/while/body/eval_jaxpr/jit(_take)/gather | solution.py:87
  85.0 2.8 %collective-permute-done.10 = bf16[4,1024]{1,0:T(4,128)(2,1)S(1)} collective-permute-done((bf16[4,1024]{1,0:T(4,128)(2,1)S(1)}, bf16[4,1024]{1,0:T(4,128)(2,1)S(1)}, u32[]{:S(2)}, u32[]{:S(2)}) %collective-permute-start.10) | collective-permute-done | bytes 8224 | tf_op jit(solution)/shard_map/ppermute | solution.py:67
  87.8 3.2 %fusion.27 = pred[1536]{0:T(1024)(128)(4,1)S(1)} fusion(pred[1536]{0:T(1024)(128)(4,1)S(1)} %get-tuple-element.253, pred[1536]{0:T(1024)(128)(4,1)S(1)} %get-tuple-element.252, pred[1536]{0:T(1024)(128)(4,1)S(1)} %get-tuple-element.251, pred[1536]{0:T(1024)(128)(4,1)S(1)} %get-tuple-element.249, pred[1536]{0:T(1024)(128)(4,1)S(1)} %get-tuple-element.250, ...), kind=kLoop, calls=%fused_computation.45 | loop fusion | flops 21504 | bytes 10757 | tf_op jit(solution)/shard_map/while/body/eval_jaxpr/jit(_take)/select_n | solution.py:87
  91.0 4.0 %collective-permute-done.11 = bf16[4,1024]{1,0:T(4,128)(2,1)S(1)} collective-permute-done((bf16[4,1024]{1,0:T(4,128)(2,1)S(1)}, bf16[4,1024]{1,0:T(4,128)(2,1)S(1)}, u32[]{:S(2)}, u32[]{:S(2)}) %collective-permute-start.11) | collective-permute-done | bytes 8224 | tf_op jit(solution)/shard_map/ppermute | solution.py:67
  95.1 7.2 %collective-permute-done.12 = bf16[4,1024]{1,0:T(4,128)(2,1)S(1)} collective-permute-done((bf16[4,1024]{1,0:T(4,128)(2,1)S(1)}, bf16[4,1024]{1,0:T(4,128)(2,1)S(1)}, u32[]{:S(2)}, u32[]{:S(2)}) %collective-permute-start.12) | collective-permute-done | bytes 8224 | tf_op jit(solution)/shard_map/ppermute | solution.py:67
  102.3 7.2 %collective-permute-done.13 = bf16[4,1024]{1,0:T(4,128)(2,1)S(1)} collective-permute-done((bf16[4,1024]{1,0:T(4,128)(2,1)S(1)}, bf16[4,1024]{1,0:T(4,128)(2,1)S(1)}, u32[]{:S(2)}, u32[]{:S(2)}) %collective-permute-start.13) | collective-permute-done | bytes 8224 | tf_op jit(solution)/shard_map/ppermute | solution.py:67
  109.6 0.1 compare_and_fusion
  109.7 7.1 %collective-permute-done.14 = bf16[4,1024]{1,0:T(4,128)(2,1)S(1)} collective-permute-done((bf16[4,1024]{1,0:T(4,128)(2,1)S(1)}, bf16[4,1024]{1,0:T(4,128)(2,1)S(1)}, u32[]{:S(2)}, u32[]{:S(2)}) %collective-permute-start.14) | collective-permute-done | bytes 8224 | tf_op jit(solution)/shard_map/ppermute | solution.py:67
  116.8 1.9 concatenate.12
  118.8 2.0 fusion.36
  120.8 1.5 fusion.12
  122.3 0.9 fusion.6
  123.3 36.3 %all-gather.4 = f32[16,64,8]{1,2,0:T(8,128)S(1)} all-gather(f32[1,64,8]{1,2,0:T(8,128)S(1)} %copy.27), channel_id=3, replica_groups=mesh['groups'=1,'kcol'=16,'qrow'=2] {'kcol'}, dimensions={0}, use_global_device_ids=true | all-gather | bytes 34816 | tf_op jit(solution)/shard_map/all_gather | solution.py:12
  159.6 39.1 %all-gather.3 = f32[16,64,8]{1,2,0:T(8,128)S(1)} all-gather(f32[1,64,8]{1,2,0:T(8,128)S(1)} %copy.26), channel_id=2, replica_groups=mesh['groups'=1,'kcol'=16,'qrow'=2] {'kcol'}, dimensions={0}, use_global_device_ids=true | all-gather | bytes 34816 | tf_op jit(solution)/shard_map/all_gather | solution.py:12
  198.7 1.0 slice.53
  199.7 21.3 %while.26 = (s32[]{:T(128)}, f32[64,8]{0,1:T(8,128)S(1)}, f32[64,8]{0,1:T(8,128)S(1)}, f32[64,8,128]{2,1,0:T(8,128)S(1)}, f32[16,64,8]{1,2,0:T(8,128)S(1)}, /*in...) while((s32[]{:T(128)}, f32[64,8]{0,1:T(8,128)S(1)}, ...), condition=%wide.region_4.5_spmd, body=%wide.region_3.4_spmd.sunk | while | flops 199685 | bytes 815247 | solution.py:17
  199.7 0.1 copy.39
  199.9 1.2 fusion.41
  201.1 0.1 copy.39
  201.3 1.2 fusion.41
  202.6 0.1 copy.39
  202.7 1.2 fusion.41
  204.2 1.2 fusion.41
  205.6 1.2 fusion.41
  207.0 1.2 fusion.41
  208.4 1.2 fusion.41
  209.8 1.2 fusion.41
  211.3 1.2 fusion.41
  212.7 1.2 fusion.41
  214.1 1.2 fusion.41
  215.5 1.2 fusion.41
  217.0 1.2 fusion.41
  218.4 1.2 fusion.41
  219.8 1.2 fusion.41
  221.3 0.6 copy.36
  (74 shorter events, 3.0 us)
Async XLA Ops:
  6.5 192.2 %all-gather.7.cloned.1.call-start = ((), (), s32[]{:S(2)}) async-start(), calls=%async_computation | async-start | bytes 4456448 | tf_op jit(solution)/shard_map/all_gather | solution.py:12
  6.5 8.8 %collective-permute-start = (bf16[4,1024]{1,0:T(4,128)(2,1)}, bf16[4,1024]{1,0:T(4,128)(2,1)S(1)}, u32[]{:S(2)}, u32[]{:S(2)}) collective-permute-start(bf16[4,1024]{1,0:T(4,128)(2,1)} %param.7), channel_id=1, source_target_pairs={{0,2},{2,4},{4,6},{6,8},{8,10},{10,12},{12,14},{14,16},{16,18},{18... | collective-permute-start | bytes 24584 | tf_op jit(solution)/shard_map/ppermute | solution.py:67
  15.3 7.2 %collective-permute-start.1 = (bf16[4,1024]{1,0:T(4,128)(2,1)S(1)}, bf16[4,1024]{1,0:T(4,128)(2,1)S(1)}, u32[]{:S(2)}, u32[]{:S(2)}) collective-permute-start(bf16[4,1024]{1,0:T(4,128)(2,1)S(1)} %collective-permute-done), channel_id=1, source_target_pairs={{0,2},{2,4},{4,6},{6,8},{8,10},{10,12},{12,14},{14,16},{16,18},{18... | collective-permute-start | bytes 24584 | tf_op jit(solution)/shard_map/ppermute | solution.py:67
  22.6 7.2 %collective-permute-start.2 = (bf16[4,1024]{1,0:T(4,128)(2,1)S(1)}, bf16[4,1024]{1,0:T(4,128)(2,1)S(1)}, u32[]{:S(2)}, u32[]{:S(2)}) collective-permute-start(bf16[4,1024]{1,0:T(4,128)(2,1)S(1)} %collective-permute-done.1), channel_id=1, source_target_pairs={{0,2},{2,4},{4,6},{6,8},{8,10},{10,12},{12,14},{14,16},{16,18},{18... | collective-permute-start | bytes 24584 | tf_op jit(solution)/shard_map/ppermute | solution.py:67
  29.8 7.2 %collective-permute-start.3 = (bf16[4,1024]{1,0:T(4,128)(2,1)S(1)}, bf16[4,1024]{1,0:T(4,128)(2,1)S(1)}, u32[]{:S(2)}, u32[]{:S(2)}) collective-permute-start(bf16[4,1024]{1,0:T(4,128)(2,1)S(1)} %collective-permute-done.2), channel_id=1, source_target_pairs={{0,2},{2,4},{4,6},{6,8},{8,10},{10,12},{12,14},{14,16},{16,18},{18... | collective-permute-start | bytes 24584 | tf_op jit(solution)/shard_map/ppermute | solution.py:67
  37.1 7.2 %collective-permute-start.4 = (bf16[4,1024]{1,0:T(4,128)(2,1)S(1)}, bf16[4,1024]{1,0:T(4,128)(2,1)S(1)}, u32[]{:S(2)}, u32[]{:S(2)}) collective-permute-start(bf16[4,1024]{1,0:T(4,128)(2,1)S(1)} %collective-permute-done.3), channel_id=1, source_target_pairs={{0,2},{2,4},{4,6},{6,8},{8,10},{10,12},{12,14},{14,16},{16,18},{18... | collective-permute-start | bytes 24584 | tf_op jit(solution)/shard_map/ppermute | solution.py:67
  44.3 7.2 %collective-permute-start.5 = (bf16[4,1024]{1,0:T(4,128)(2,1)S(1)}, bf16[4,1024]{1,0:T(4,128)(2,1)S(1)}, u32[]{:S(2)}, u32[]{:S(2)}) collective-permute-start(bf16[4,1024]{1,0:T(4,128)(2,1)S(1)} %collective-permute-done.4), channel_id=1, source_target_pairs={{0,2},{2,4},{4,6},{6,8},{8,10},{10,12},{12,14},{14,16},{16,18},{18... | collective-permute-start | bytes 24584 | tf_op jit(solution)/shard_map/ppermute | solution.py:67
  51.6 7.2 %collective-permute-start.6 = (bf16[4,1024]{1,0:T(4,128)(2,1)S(1)}, bf16[4,1024]{1,0:T(4,128)(2,1)S(1)}, u32[]{:S(2)}, u32[]{:S(2)}) collective-permute-start(bf16[4,1024]{1,0:T(4,128)(2,1)S(1)} %collective-permute-done.5), channel_id=1, source_target_pairs={{0,2},{2,4},{4,6},{6,8},{8,10},{10,12},{12,14},{14,16},{16,18},{18... | collective-permute-start | bytes 24584 | tf_op jit(solution)/shard_map/ppermute | solution.py:67
  58.8 7.2 %collective-permute-start.7 = (bf16[4,1024]{1,0:T(4,128)(2,1)S(1)}, bf16[4,1024]{1,0:T(4,128)(2,1)S(1)}, u32[]{:S(2)}, u32[]{:S(2)}) collective-permute-start(bf16[4,1024]{1,0:T(4,128)(2,1)S(1)} %collective-permute-done.6), channel_id=1, source_target_pairs={{0,2},{2,4},{4,6},{6,8},{8,10},{10,12},{12,14},{14,16},{16,18},{18... | collective-permute-start | bytes 24584 | tf_op jit(solution)/shard_map/ppermute | solution.py:67
  66.1 7.2 %collective-permute-start.8 = (bf16[4,1024]{1,0:T(4,128)(2,1)S(1)}, bf16[4,1024]{1,0:T(4,128)(2,1)S(1)}, u32[]{:S(2)}, u32[]{:S(2)}) collective-permute-start(bf16[4,1024]{1,0:T(4,128)(2,1)S(1)} %collective-permute-done.7), channel_id=1, source_target_pairs={{0,2},{2,4},{4,6},{6,8},{8,10},{10,12},{12,14},{14,16},{16,18},{18... | collective-permute-start | bytes 24584 | tf_op jit(solution)/shard_map/ppermute | solution.py:67
  73.3 7.2 %collective-permute-start.9 = (bf16[4,1024]{1,0:T(4,128)(2,1)S(1)}, bf16[4,1024]{1,0:T(4,128)(2,1)S(1)}, u32[]{:S(2)}, u32[]{:S(2)}) collective-permute-start(bf16[4,1024]{1,0:T(4,128)(2,1)S(1)} %collective-permute-done.8), channel_id=1, source_target_pairs={{0,2},{2,4},{4,6},{6,8},{8,10},{10,12},{12,14},{14,16},{16,18},{18... | collective-permute-start | bytes 24584 | tf_op jit(solution)/shard_map/ppermute | solution.py:67
  80.6 7.2 %collective-permute-start.10 = (bf16[4,1024]{1,0:T(4,128)(2,1)S(1)}, bf16[4,1024]{1,0:T(4,128)(2,1)S(1)}, u32[]{:S(2)}, u32[]{:S(2)}) collective-permute-start(bf16[4,1024]{1,0:T(4,128)(2,1)S(1)} %collective-permute-done.9), channel_id=1, source_target_pairs={{0,2},{2,4},{4,6},{6,8},{8,10},{10,12},{12,14},{14,16},{16,18},{18... | collective-permute-start | bytes 24584 | tf_op jit(solution)/shard_map/ppermute | solution.py:67
  87.8 7.2 %collective-permute-start.11 = (bf16[4,1024]{1,0:T(4,128)(2,1)S(1)}, bf16[4,1024]{1,0:T(4,128)(2,1)S(1)}, u32[]{:S(2)}, u32[]{:S(2)}) collective-permute-start(bf16[4,1024]{1,0:T(4,128)(2,1)S(1)} %collective-permute-done.10), channel_id=1, source_target_pairs={{0,2},{2,4},{4,6},{6,8},{8,10},{10,12},{12,14},{14,16},{16,18},{18... | collective-permute-start | bytes 24584 | tf_op jit(solution)/shard_map/ppermute | solution.py:67
  95.1 7.2 %collective-permute-start.12 = (bf16[4,1024]{1,0:T(4,128)(2,1)S(1)}, bf16[4,1024]{1,0:T(4,128)(2,1)S(1)}, u32[]{:S(2)}, u32[]{:S(2)}) collective-permute-start(bf16[4,1024]{1,0:T(4,128)(2,1)S(1)} %collective-permute-done.11), channel_id=1, source_target_pairs={{0,2},{2,4},{4,6},{6,8},{8,10},{10,12},{12,14},{14,16},{16,18},{18... | collective-permute-start | bytes 24584 | tf_op jit(solution)/shard_map/ppermute | solution.py:67
  102.3 7.2 %collective-permute-start.13 = (bf16[4,1024]{1,0:T(4,128)(2,1)S(1)}, bf16[4,1024]{1,0:T(4,128)(2,1)S(1)}, u32[]{:S(2)}, u32[]{:S(2)}) collective-permute-start(bf16[4,1024]{1,0:T(4,128)(2,1)S(1)} %collective-permute-done.12), channel_id=1, source_target_pairs={{0,2},{2,4},{4,6},{6,8},{8,10},{10,12},{12,14},{14,16},{16,18},{18... | collective-permute-start | bytes 24584 | tf_op jit(solution)/shard_map/ppermute | solution.py:67
  109.6 7.2 %collective-permute-start.14 = (bf16[4,1024]{1,0:T(4,128)(2,1)S(1)}, bf16[4,1024]{1,0:T(4,128)(2,1)S(1)}, u32[]{:S(2)}, u32[]{:S(2)}) collective-permute-start(bf16[4,1024]{1,0:T(4,128)(2,1)S(1)} %collective-permute-done.13), channel_id=1, source_target_pairs={{0,2},{2,4},{4,6},{6,8},{8,10},{10,12},{12,14},{14,16},{16,18},{18... | collective-permute-start | bytes 24584 | tf_op jit(solution)/shard_map/ppermute | solution.py:67
  118.7 2.1 copy-start
Sparse Core Ops, SparseCore 0:
  122.4 72.0 all-gather.6
